TPU v7x, 32 devices: a whole 2x2x4 slice. The times are simulated.
32 devices in a mesh: row: 8 (over z, y), col: 4 (over x, core).
Axes of the slice: x: 2, y: 2, z: 4, core: 2. Of those that a mesh axis runs over, the one named last changes fastest.
Arguments:
- eigvecs: bfloat16 [131072, 4096], P('row', 'col'), may hold values from -6 to 6
- reflectors: bfloat16 [131072, 1024], P('row', 'col'), may hold values from -0.046875 to 0.046875
- t_factors: float32 [1024, 256], P('col'), as said below
- owners: int32 [2], replicated, may hold values from 0 to 3, as said below
- band_owner: int32 [1024, 1], P('row'), may hold values from 0 to 7; in each aligned block of 128 rows (0 to 127, 128 to 255, ...) at most 20 rows name the same one
Outputs:
- owned: bfloat16 [163840, 4096], P('row', 'col')
Inputs may be any that keep to these rules, and one draw needn't show every extreme that they name: `owners`: the 2 entries are different column indices, and one of them is the last column index. `t_factors`: each block of 256 rows is upper triangular. `band_owner`: among the 128 rows of one index of row, no owner is named more than 20 times.
All inputs are finite; a program needn't handle non-finite values.
Results may differ from a plain program's by a relative error of at most 0.015.
Values may be sent and summed in bfloat16 or wider, within the bound.
No kernel may reach another device: no remote copies, remote signals or barrier semaphores. Data moves between devices by JAX's collectives and lax.ppermute only.
A program may use at most 384 MiB of HBM per device.

v0:
```python
import jax
import jax.numpy as jnp
from jax import lax
from jax.sharding import PartitionSpec as P

contract_rows = (((0,), (0,)), ((), ()))


def broadcast(value, axis, source):
    kept = jnp.where(lax.axis_index(axis) == source, value, 0).astype(value.dtype)
    return lax.psum(kept, axis)


def fetch_panel(reflectors, t_factors, owners, which):
    return (
        broadcast(reflectors, "col", owners[which]),
        broadcast(t_factors.astype(jnp.bfloat16), "col", owners[which]).astype(t_factors.dtype),
    )


def project(panel_rows, field):
    if field.dtype == jnp.float32:
        return lax.dot_general(
            panel_rows.astype(jnp.float32),
            field,
            contract_rows,
            precision=lax.Precision.HIGHEST,
            preferred_element_type=jnp.float32,
        )
    return lax.dot_general(panel_rows, field, contract_rows, preferred_element_type=jnp.float32)


def settle(partial_value, triangle):
    products = lax.psum(partial_value.astype(jnp.bfloat16), "row").astype(jnp.float32)
    return jnp.dot(triangle, products, precision=lax.Precision.HIGHEST).astype(jnp.bfloat16)


def pack_slots(finished, slot_index, slot_total):
    block_count = finished.shape[0] // 128
    blocks = finished.reshape(block_count, 128, finished.shape[1])
    return jnp.zeros((slot_total, 128, finished.shape[1]), jnp.bfloat16).at[slot_index].set(blocks)


def body(eigvecs, reflectors, t_factors, owners, band_owner):
    field = eigvecs
    for which in range(2):
        panel_rows, triangle = fetch_panel(reflectors, t_factors, owners, which)
        update = settle(project(panel_rows, field), triangle)
        if which == 0:
            field = field.astype(jnp.float32) - jnp.dot(
                panel_rows, update, preferred_element_type=jnp.float32
            )
        else:
            base_field = field
            last_rows = panel_rows
            last_update = update
    block_count = base_field.shape[0] // 128
    local_width = base_field.shape[1]
    row_count = lax.axis_size("row")
    capacity = (5 * block_count + 4 * row_count - 1) // (4 * row_count)
    slot_total = row_count * capacity
    owner_of = band_owner[:, 0]
    position = jnp.arange(block_count, dtype=jnp.int32)
    shared = (owner_of[:, None] == owner_of[None, :]) & (position[None, :] < position[:, None])
    order_in = jnp.sum(shared.astype(jnp.int32), axis=1)
    slot_index = owner_of * capacity + order_in
    finished = (
        base_field - jnp.dot(last_rows, last_update, preferred_element_type=jnp.float32)
    ).astype(jnp.bfloat16)
    arrived = lax.all_to_all(
        pack_slots(finished, slot_index, slot_total), "row", split_axis=0, concat_axis=0, tiled=True
    )
    return arrived.reshape(slot_total * 128, local_width)


def solution(mesh):
    in_specs = (P("row", "col"), P("row", "col"), P("col", None), P(), P("row", None))
    out_specs = P("row", "col")
    return jax.shard_map(body, mesh=mesh, in_specs=in_specs, out_specs=out_specs, check_vma=False)
```

profile of v0, /device:TPU:0, one launch (start us, length us, event | category | flops | bytes accessed | tf_op | source)
XLA Modules:
  0.0 1645.3 jit_solution(16833816957001968534)
XLA Ops:
  6.5 0.0 all-reduce.9.cloned.1.call-start
  6.5 1.3 fusion.4
  9.1 9.5 broadcast_select_fusion
  18.6 1.7 broadcast_select_fusion.2
  20.3 0.0 all-reduce.9.cloned.1.call-update
  20.3 0.0 all-reduce.5.cloned.1.call-start
  20.4 295.8 %all-reduce.9.cloned.1.call-done = (bf16[16384,256]{1,0:T(8,128)(2,1)}, bf16[256,256]{1,0:T(8,128)(2,1)}, bf16[16384,256]{1,0:T(8,128)(2,1)}, bf16[256,256]{1,0:T(8,128)(2,1)}) async-done(((bf16[16384,256]{1,0:T(8,128)(2,1)}, bf16[256,256]{1,0:T(8,128)(2,1)}, bf16[16384,256]{1,0:T(8,128)(2,1)}, bf16[256,256]{1,0:T(8,128)(2,1)}), (bf16[16384,256]{1,0:T(8,128)(2,1)}, bf16[256,256]{1,0:T(8,128)(2,1)}, ...) | async-done | bytes 17039376 | tf_op jit(solution)/shard_map/psum | solution.py:11
  316.1 0.0 copy-start.1
  316.1 18.2 %convolution_convert_fusion.2 = bf16[256,1024]{1,0:T(8,128)(2,1)} fusion(bf16[16384,256]{1,0:T(8,128)(2,1)} %get-tuple-element.5, bf16[16384,1024]{1,0:T(8,128)(2,1)} %param.5), kind=kOutput, calls=%fused_computation.9 | convolution fusion | flops 8590196736 | bytes 42467328 | tf_op jit(solution)/shard_map/dot_general | solution.py:30
  334.3 0.0 all-reduce.5.cloned.1.call-update
  334.3 0.2 all-reduce.7.cloned.1.call-start
  334.6 72.6 %all-reduce.5.cloned.1.call-done = bf16[256,1024]{1,0:T(8,128)(2,1)} async-done(((bf16[256,1024]{1,0:T(8,128)(2,1)}), bf16[256,1024]{1,0:T(8,128)(2,1)}) %all-reduce.5.cloned.1.call-update) | async-done | bytes 524304 | tf_op jit(solution)/shard_map/psum | solution.py:34
  407.1 0.0 copy-done.1
  407.2 1.3 convolution_convert_fusion.1
  408.5 26.6 %fusion.5 = f32[16384,1024]{1,0:T(8,128)} fusion(bf16[16384,256]{1,0:T(8,128)(2,1)} %get-tuple-element.5, bf16[256,1024]{1,0:T(8,128)(2,1)S(1)} %convolution_convert_fusion.1), kind=kOutput, calls=%fused_computation.19 | convolution fusion | flops 8589934592 | bytes 76021760 | tf_op jit(solution)/shard_map/dot_general | solution.py:50
  435.1 0.0 copy-start.2
  435.1 0.0 copy-start
  435.1 45.6 %fusion.1 = bf16[256,1024]{1,0:T(8,128)(2,1)} fusion(bf16[16384,256]{1,0:T(8,128)(2,1)} %get-tuple-element.7, f32[16384,1024]{1,0:T(8,128)} %fusion.5, bf16[16384,1024]{1,0:T(8,128)(2,1)} %param.5), kind=kOutput, calls=%fused_computation.8 | convolution fusion | flops 51573424128 | bytes 109576192 | tf_op jit(solution)/shard_map/dot_general | solution.py:23
  480.7 0.0 all-reduce.7.cloned.1.call-update
  480.7 0.0 copy-done.2
  480.7 0.2 convert_reduce_fusion
  480.9 71.8 %all-reduce.7.cloned.1.call-done = bf16[256,1024]{1,0:T(8,128)(2,1)} async-done(((bf16[256,1024]{1,0:T(8,128)(2,1)}), bf16[256,1024]{1,0:T(8,128)(2,1)}) %all-reduce.7.cloned.1.call-update) | async-done | bytes 524304 | tf_op jit(solution)/shard_map/psum | solution.py:34
  552.7 0.0 copy-done
  552.7 1.3 convolution_convert_fusion
  554.0 46.4 %subtract_convert_fusion = bf16[16384,1024]{1,0:T(8,128)(2,1)} fusion(f32[16384,1024]{1,0:T(8,128)} %fusion.5, bf16[16384,1024]{1,0:T(8,128)(2,1)} %param.5, bf16[16384,256]{1,0:T(8,128)(2,1)} %get-tuple-element.7, bf16[256,1024]{1,0:T(8,128)(2,1)S(1)} %convolution_convert_fusion), kind=kOutput, calls=%fused_computation.1 | convolution fusion | flops 8657043456 | bytes 143130624 | tf_op jit(solution)/shard_map/dot_general | solution.py:68
  600.5 13.7 broadcast_in_dim.16
  614.2 82.9 %scatter_fusion = bf16[160,128,1024]{2,1,0:T(8,128)(2,1)} fusion(bf16[160,128,1024]{2,1,0:T(8,128)(2,1)} %broadcast_in_dim.16, s32[128]{0:T(128)S(1)} %fusion.3, bf16[128,128,1024]{2,1,0:T(8,128)(2,1)} %bitcast.23), kind=kCustom, calls=%fused_computation | custom fusion | bytes 100663808 | tf_op jit(solution)/shard_map/scatter | solution.py:41
  697.0 913.6 %all_to_all.5 = bf16[160,128,1024]{2,1,0:T(8,128)(2,1)} all-to-all(bf16[160,128,1024]{2,1,0:T(8,128)(2,1)} %scatter_fusion), channel_id=1, replica_groups=mesh['row'=8,'col'=4] {'row'}, dimensions={0} | all-to-all | bytes 83886080 | tf_op jit(solution)/shard_map/all_to_all | solution.py:70
  1610.6 28.2 %copy.14 = bf16[20480,1024]{1,0:T(8,128)(2,1)} copy(bf16[20480,1024]{1,0:T(8,128)(2,1)} %bitcast.22) | data formatting | bytes 83886080
  (1 shorter events, 0.0 us)
Async XLA Ops:
  6.5 309.6 %all-reduce.9.cloned.1.call-start = ((), (), s32[]{:S(2)}) async-start(), calls=%async_computation.3 | async-start | bytes 34078720 | tf_op jit(solution)/shard_map/psum | solution.py:11
  20.3 386.8 %all-reduce.5.cloned.1.call-start = ((), (), s32[]{:S(2)}) async-start(), calls=%async_computation.1 | async-start | bytes 1048576 | tf_op jit(solution)/shard_map/psum | solution.py:34
  316.1 91.0 %copy-start.1 = (bf16[256,256]{1,0:T(8,128)(2,1)S(1)}, bf16[256,256]{1,0:T(8,128)(2,1)}, u32[]{:S(2)}) copy-start(bf16[256,256]{1,0:T(8,128)(2,1)} %get-tuple-element.6) | copy-start | bytes 393220
  334.3 218.3 %all-reduce.7.cloned.1.call-start = ((), (), s32[]{:S(2)}) async-start(), calls=%async_computation.2 | async-start | bytes 1048576 | tf_op jit(solution)/shard_map/psum | solution.py:34
  435.1 45.6 %copy-start.2 = (s32[128,1]{0,1:T(1,128)S(1)}, s32[128,1]{0,1:T(1,128)}, u32[]{:S(2)}) copy-start(s32[128,1]{0,1:T(1,128)} %param.9) | copy-start | bytes 1540
  435.1 117.6 %copy-start = (bf16[256,256]{1,0:T(8,128)(2,1)S(1)}, bf16[256,256]{1,0:T(8,128)(2,1)}, u32[]{:S(2)}) copy-start(bf16[256,256]{1,0:T(8,128)(2,1)} %get-tuple-element.8) | copy-start | bytes 393220
Sparse Core Ops, SparseCore 0:
  20.5 295.6 all-reduce.8
  334.5 72.6 all-reduce.4
  480.8 71.8 all-reduce.6
where the time goes:
time: 1650 us
  blocking collectives  914 us (55%)
  waiting for transfers between devices  440 us (27%)
  matrix products  139 us (8%)
  local copies, waits for them, and re-layouts  126 us (8%)
    all_to_all x1, blocking collectives, body(): lax.all_to_all(pack_slots(finished, slot_index, slot_total), 'row', split...  914 us
    psum x1, waiting for transfers between devices, broadcast(): return lax.psum(kept, axis)  296 us
    psum x2, waiting for transfers between devices, settle(): lax.psum(partial_value.astype(jnp.bfloat16), 'row').astype(jnp.float32)  144 us
    scatter x1, local copies, waits for them, and re-layouts, pack_slots(): jnp.zeros((slot_total, 128, finished.shape[1]), jnp.bfloat16).at[slot_index]  82.9 us
    dot_general x1, matrix products, body(): jnp.dot(last_rows, last_update, preferred_element_type=jnp.float32)  46.4 us
    dot_general x1, matrix products, project(): lax.dot_general(panel_rows.astype(jnp.float32), field, contract_rows, pre...  45.6 us
  transfers between devices with their start and end apart: 3, of which 3 were waited for; matrix products, arithmetic and copies ran while one was open for 0% of the time, Pallas kernels for 0%

commit v1 on v0

--- a/solution.py
+++ b/solution.py
@@ -4,6 +4,28 @@
 from jax.sharding import PartitionSpec as P
 
 contract_rows = (((0,), (0,)), ((), ()))
+
+
+def in_blocks(x, dim, size):
+    before, after = (x.shape[:dim], x.shape[dim + 1 :])
+    return jnp.moveaxis(x.reshape(*before, size, -1, *after), dim, 0)
+
+
+def in_order(blocks, dim):
+    shape = list(blocks.shape[1:])
+    shape[dim] *= blocks.shape[0]
+    return jnp.moveaxis(blocks, 0, dim).reshape(shape)
+
+
+def sent_to_each(shard, axis, split_dim, concat_dim):
+    size, mine = (lax.axis_size(axis), lax.axis_index(axis))
+    pieces = in_blocks(shard, split_dim, size)
+    outs = [pieces[mine]]
+    for step in range(1, size):
+        sent = pieces[(mine + step) % size]
+        outs.append(lax.ppermute(sent, axis, [(i, (i + step) % size) for i in range(size)]))
+    pieces = jnp.stack(outs)[(mine - jnp.arange(size)) % size]
+    return in_order(pieces, concat_dim)
 
 
 def broadcast(value, axis, source):
@@ -67,9 +89,7 @@
     finished = (
         base_field - jnp.dot(last_rows, last_update, preferred_element_type=jnp.float32)
     ).astype(jnp.bfloat16)
-    arrived = lax.all_to_all(
-        pack_slots(finished, slot_index, slot_total), "row", split_axis=0, concat_axis=0, tiled=True
-    )
+    arrived = sent_to_each(pack_slots(finished, slot_index, slot_total), "row", 0, 0)
     return arrived.reshape(slot_total * 128, local_width)
 
 

time: 1650 us -> 1740 us (1.055)
  the two profiles are of different devices: /device:TPU:0 before, /device:TPU:30 now
where the time goes in v1:
time: 1740 us
  waiting for transfers between devices  1310 us (75%)
  local copies, waits for them, and re-layouts  229 us (13%)
  matrix products  140 us (8%)
  other arithmetic  38.7 us (2%)
    ppermute x7, waiting for transfers between devices, sent_to_each(): lax.ppermute(sent, axis, [(i, (i + step) % size) for i in range(size)])  871 us
    psum x1, waiting for transfers between devices, broadcast(): return lax.psum(kept, axis)  293 us
    psum x2, waiting for transfers between devices, settle(): lax.psum(partial_value.astype(jnp.bfloat16), 'row').astype(jnp.float32)  144 us
    scatter x1, local copies, waits for them, and re-layouts, pack_slots(): jnp.zeros((slot_total, 128, finished.shape[1]), jnp.bfloat16).at[slot_index]  82.9 us
    gather x5, local copies, waits for them, and re-layouts, sent_to_each(): pieces = jnp.stack(outs)[(mine - jnp.arange(size)) % size]  68 us
    dot_general x1, matrix products, body(): jnp.dot(last_rows, last_update, preferred_element_type=jnp.float32)  46.4 us
    dot_general x1, matrix products, project(): lax.dot_general(panel_rows.astype(jnp.float32), field, contract_rows, pre...  45.6 us
  transfers between devices with their start and end apart: 10, of which 7 were waited for; matrix products, arithmetic and copies ran while one was open for 2% of the time, Pallas kernels for 0%

profile of v1, /device:TPU:30, one launch (start us, length us, event | category | flops | bytes accessed | tf_op | source)
XLA Modules:
  0.0 1736.9 jit_solution(11671732305424454957)
XLA Ops:
  6.5 1.3 fusion.7
  9.1 9.5 broadcast_select_fusion
  18.6 0.7 broadcast_select_fusion.2
  19.4 0.0 all-reduce.9.cloned.1.call-update
  19.4 0.0 all-reduce.5.cloned.1.call-start
  19.4 292.9 %all-reduce.9.cloned.1.call-done = (bf16[16384,256]{1,0:T(8,128)(2,1)}, bf16[256,256]{1,0:T(8,128)(2,1)}, bf16[16384,256]{1,0:T(8,128)(2,1)}, bf16[256,256]{1,0:T(8,128)(2,1)}) async-done(((bf16[16384,256]{1,0:T(8,128)(2,1)}, bf16[256,256]{1,0:T(8,128)(2,1)}, bf16[16384,256]{1,0:T(8,128)(2,1)}, bf16[256,256]{1,0:T(8,128)(2,1)}), (bf16[16384,256]{1,0:T(8,128)(2,1)}, bf16[256,256]{1,0:T(8,128)(2,1)}, ...) | async-done | bytes 17039376 | tf_op jit(solution)/shard_map/psum | solution.py:33
  312.3 18.2 %convolution_convert_fusion.2 = bf16[256,1024]{1,0:T(8,128)(2,1)} fusion(bf16[16384,256]{1,0:T(8,128)(2,1)} %get-tuple-element.5, bf16[16384,1024]{1,0:T(8,128)(2,1)} %param.5), kind=kOutput, calls=%fused_computation.28 | convolution fusion | flops 8590196736 | bytes 42467328 | tf_op jit(solution)/shard_map/dot_general | solution.py:52
  330.5 0.0 all-reduce.5.cloned.1.call-update
  330.5 0.0 all-reduce.7.cloned.1.call-start
  330.6 72.1 %all-reduce.5.cloned.1.call-done = bf16[256,1024]{1,0:T(8,128)(2,1)} async-done(((bf16[256,1024]{1,0:T(8,128)(2,1)}), bf16[256,1024]{1,0:T(8,128)(2,1)}) %all-reduce.5.cloned.1.call-update) | async-done | bytes 524304 | tf_op jit(solution)/shard_map/psum | solution.py:56
  402.7 1.3 convolution_convert_fusion.1
  404.0 26.8 %fusion.8 = f32[16384,1024]{1,0:T(8,128)} fusion(bf16[16384,256]{1,0:T(8,128)(2,1)} %get-tuple-element.5, bf16[256,1024]{1,0:T(8,128)(2,1)S(1)} %convolution_convert_fusion.1), kind=kOutput, calls=%fused_computation.46 | convolution fusion | flops 8589934592 | bytes 76021760 | tf_op jit(solution)/shard_map/dot_general | solution.py:72
  430.8 45.6 %fusion.1 = bf16[256,1024]{1,0:T(8,128)(2,1)} fusion(bf16[16384,256]{1,0:T(8,128)(2,1)} %get-tuple-element.7, f32[16384,1024]{1,0:T(8,128)} %fusion.8, bf16[16384,1024]{1,0:T(8,128)(2,1)} %param.5), kind=kOutput, calls=%fused_computation.27 | convolution fusion | flops 51573424128 | bytes 109576192 | tf_op jit(solution)/shard_map/dot_general | solution.py:45
  476.4 0.0 all-reduce.7.cloned.1.call-update
  476.5 0.2 convert_reduce_fusion
  476.7 71.7 %all-reduce.7.cloned.1.call-done = bf16[256,1024]{1,0:T(8,128)(2,1)} async-done(((bf16[256,1024]{1,0:T(8,128)(2,1)}), bf16[256,1024]{1,0:T(8,128)(2,1)}) %all-reduce.7.cloned.1.call-update) | async-done | bytes 524304 | tf_op jit(solution)/shard_map/psum | solution.py:56
  548.4 1.3 convolution_convert_fusion
  549.7 46.4 %subtract_convert_fusion = bf16[16384,1024]{1,0:T(8,128)(2,1)} fusion(f32[16384,1024]{1,0:T(8,128)} %fusion.8, bf16[16384,1024]{1,0:T(8,128)(2,1)} %param.5, bf16[16384,256]{1,0:T(8,128)(2,1)} %get-tuple-element.7, bf16[256,1024]{1,0:T(8,128)(2,1)S(1)} %convolution_convert_fusion), kind=kOutput, calls=%fused_computation.4 | convolution fusion | flops 8657043456 | bytes 143130624 | tf_op jit(solution)/shard_map/dot_general | solution.py:90
  596.1 13.7 broadcast_in_dim.17
  609.8 82.9 %scatter_fusion = bf16[160,128,1024]{2,1,0:T(8,128)(2,1)} fusion(bf16[160,128,1024]{2,1,0:T(8,128)(2,1)} %broadcast_in_dim.17, s32[128]{0:T(128)S(1)} %fusion.4, bf16[128,128,1024]{2,1,0:T(8,128)(2,1)} %bitcast.54), kind=kCustom, calls=%fused_computation.3 | custom fusion | bytes 100663808 | tf_op jit(solution)/shard_map/scatter | solution.py:63
  692.7 28.5 %dynamic-slice_bitcast_fusion = (bf16[20,128,1024]{2,1,0:T(8,128)(2,1)}, bf16[20,128,1024]{2,1,0:T(8,128)(2,1)}, bf16[20,128,1024]{2,1,0:T(8,128)(2,1)}, bf16[20...) fusion(bf16[8,20,128,1024]{3,2,1,0:T(8,128)(2,1)} %bitcast.53, ...), kind=kLoop, calls=%fused_computation.17 | loop fusion | bytes 83886112 | tf_op jit(solution)/shard_map/squeeze | solution.py:25
  721.2 2.3 collective-permute-start
  723.4 1.0 collective-permute-start.1
  724.4 1.1 collective-permute-start.2
  725.6 1.5 collective-permute-start.3
  727.1 1.2 collective-permute-start.4
  728.3 109.0 %collective-permute-done = bf16[20,128,1024]{2,1,0:T(8,128)(2,1)S(1)} collective-permute-done((bf16[20,128,1024]{2,1,0:T(8,128)(2,1)}, bf16[20,128,1024]{2,1,0:T(8,128)(2,1)S(1)}, u32[]{:S(2)}, u32[]{:S(2)}) %collective-permute-start) | collective-permute-done | bytes 5242912 | tf_op jit(solution)/shard_map/ppermute | solution.py:26
  837.3 2.4 copy-done
  839.6 0.6 collective-permute-start.5
  840.2 109.4 %collective-permute-done.1 = bf16[20,128,1024]{2,1,0:T(8,128)(2,1)S(1)} collective-permute-done((bf16[20,128,1024]{2,1,0:T(8,128)(2,1)}, bf16[20,128,1024]{2,1,0:T(8,128)(2,1)S(1)}, u32[]{:S(2)}, u32[]{:S(2)}) %collective-permute-start.1) | collective-permute-done | bytes 5242912 | tf_op jit(solution)/shard_map/ppermute | solution.py:26
  949.6 2.3 copy-done.1
  951.9 0.0 collective-permute-start.6
  952.0 5.6 bitcast_dynamic-update-slice_fusion.6
  957.6 5.7 bitcast_dynamic-update-slice_fusion.5
  963.3 98.8 %collective-permute-done.2 = bf16[20,128,1024]{2,1,0:T(8,128)(2,1)} collective-permute-done((bf16[20,128,1024]{2,1,0:T(8,128)(2,1)}, bf16[20,128,1024]{2,1,0:T(8,128)(2,1)}, u32[]{:S(2)}, u32[]{:S(2)}) %collective-permute-start.2) | collective-permute-done | bytes 5242912 | tf_op jit(solution)/shard_map/ppermute | solution.py:26
  1062.0 5.6 bitcast_dynamic-update-slice_fusion.4
  1067.6 553.8 %collective-permute-done.3 = bf16[20,128,1024]{2,1,0:T(8,128)(2,1)S(1)} collective-permute-done((bf16[20,128,1024]{2,1,0:T(8,128)(2,1)}, bf16[20,128,1024]{2,1,0:T(8,128)(2,1)S(1)}, u32[]{:S(2)}, u32[]{:S(2)}) %collective-permute-start.3) | collective-permute-done | bytes 5242912 | tf_op jit(solution)/shard_map/ppermute | solution.py:26
  1621.4 3.2 bitcast_dynamic-update-slice_fusion.3
  1624.6 3.2 bitcast_dynamic-update-slice_fusion.2
  1627.9 0.0 collective-permute-done.5
  1627.9 3.1 bitcast_dynamic-update-slice_fusion.1
  1631.0 3.1 bitcast_dynamic-update-slice_fusion
  1634.1 23.3 %fusion.6 = (bf16[8,20,128,384]{3,2,1,0:T(8,128)(2,1)}, bf16[8,20,128,384]{3,2,1,0:T(8,128)(2,1)}) fusion(bf16[8,20,128,1024]{3,2,1,0:T(8,128)(2,1)} %bitcast_dynamic-update-slice_fusion), kind=kLoop, calls=%fused_computation.44 | loop fusion | bytes 62914560 | tf_op jit(solution)/shard_map/gather | solution.py:27
  1657.4 9.6 mini-gather-slice.5
  1667.0 12.8 gather_fusion
  1679.8 12.8 gather_fusion.1
  1692.6 9.5 gather_fusion.2
  1702.1 28.3 %pad_maximum_fusion = bf16[8,20,128,1024]{3,2,1,0:T(8,128)(2,1)} fusion(bf16[8,20,128,256]{3,2,1,0:T(8,128)(2,1)} %gather_fusion.2, bf16[8,20,128,384]{3,2,1,0:T(8,128)(2,1)} %gather_fusion.1, bf16[8,20,128,384]{3,2,1,0:T(8,128)(2,1)} %gather_fusion), kind=kLoop, calls=%fused_computation.7 | loop fusion | flops 125829120 | bytes 83886080
  (16 shorter events, 0.1 us)
Async XLA Ops:
  6.5 12.1 copy-start.2
  6.5 305.8 %all-reduce.9.cloned.1.call-start = ((), (), s32[]{:S(2)}) async-start(), calls=%async_computation.2 | async-start | bytes 34078720 | tf_op jit(solution)/shard_map/psum | solution.py:33
  19.4 383.3 %all-reduce.5.cloned.1.call-start = ((), (), s32[]{:S(2)}) async-start(), calls=%async_computation | async-start | bytes 1048576 | tf_op jit(solution)/shard_map/psum | solution.py:56
  312.3 90.4 %copy-start.4 = (bf16[256,256]{1,0:T(8,128)(2,1)S(1)}, bf16[256,256]{1,0:T(8,128)(2,1)}, u32[]{:S(2)}) copy-start(bf16[256,256]{1,0:T(8,128)(2,1)} %get-tuple-element.6) | copy-start | bytes 393220
  330.5 217.9 %all-reduce.7.cloned.1.call-start = ((), (), s32[]{:S(2)}) async-start(), calls=%async_computation.1 | async-start | bytes 1048576 | tf_op jit(solution)/shard_map/psum | solution.py:56
  430.8 45.7 %copy-start.5 = (s32[128,1]{0,1:T(1,128)S(1)}, s32[128,1]{0,1:T(1,128)}, u32[]{:S(2)}) copy-start(s32[128,1]{0,1:T(1,128)} %param.9) | copy-start | bytes 1540
  430.8 117.6 %copy-start.3 = (bf16[256,256]{1,0:T(8,128)(2,1)S(1)}, bf16[256,256]{1,0:T(8,128)(2,1)}, u32[]{:S(2)}) copy-start(bf16[256,256]{1,0:T(8,128)(2,1)} %get-tuple-element.8) | copy-start | bytes 393220
  721.2 116.1 %collective-permute-start = (bf16[20,128,1024]{2,1,0:T(8,128)(2,1)}, bf16[20,128,1024]{2,1,0:T(8,128)(2,1)S(1)}, u32[]{:S(2)}, u32[]{:S(2)}) collective-permute-start(bf16[20,128,1024]{2,1,0:T(8,128)(2,1)} %get-tuple-element.17), channel_id=1, source_target_pairs={{0,4},{4,8},{8,12},{12,16},{16,20},{20,24},{24,28},{28,0},{1,5},{5... | collective-permute-start | bytes 15728648 | tf_op jit(solution)/shard_map/ppermute | solution.py:26
  723.4 226.2 %collective-permute-start.1 = (bf16[20,128,1024]{2,1,0:T(8,128)(2,1)}, bf16[20,128,1024]{2,1,0:T(8,128)(2,1)S(1)}, u32[]{:S(2)}, u32[]{:S(2)}) collective-permute-start(bf16[20,128,1024]{2,1,0:T(8,128)(2,1)} %get-tuple-element.16), channel_id=1, source_target_pairs={{0,8},{4,12},{8,16},{12,20},{16,24},{20,28},{24,0},{28,4},{1,9},{5... | collective-permute-start | bytes 15728648 | tf_op jit(solution)/shard_map/ppermute | solution.py:26
  724.4 337.6 %collective-permute-start.2 = (bf16[20,128,1024]{2,1,0:T(8,128)(2,1)}, bf16[20,128,1024]{2,1,0:T(8,128)(2,1)}, u32[]{:S(2)}, u32[]{:S(2)}) collective-permute-start(bf16[20,128,1024]{2,1,0:T(8,128)(2,1)} %get-tuple-element.15), channel_id=1, source_target_pairs={{0,12},{4,16},{8,20},{12,24},{16,28},{20,0},{24,4},{28,8},{1,13},{... | collective-permute-start | bytes 15728648 | tf_op jit(solution)/shard_map/ppermute | solution.py:26
  725.6 895.9 %collective-permute-start.3 = (bf16[20,128,1024]{2,1,0:T(8,128)(2,1)}, bf16[20,128,1024]{2,1,0:T(8,128)(2,1)S(1)}, u32[]{:S(2)}, u32[]{:S(2)}) collective-permute-start(bf16[20,128,1024]{2,1,0:T(8,128)(2,1)} %get-tuple-element.14), channel_id=1, source_target_pairs={{0,16},{4,20},{8,24},{12,28},{16,0},{20,4},{24,8},{28,12},{1,17},{... | collective-permute-start | bytes 15728648 | tf_op jit(solution)/shard_map/ppermute | solution.py:26
  727.1 897.5 %collective-permute-start.4 = (bf16[20,128,1024]{2,1,0:T(8,128)(2,1)}, bf16[20,128,1024]{2,1,0:T(8,128)(2,1)S(1)}, u32[]{:S(2)}, u32[]{:S(2)}) collective-permute-start(bf16[20,128,1024]{2,1,0:T(8,128)(2,1)} %get-tuple-element.13), channel_id=1, source_target_pairs={{0,20},{4,24},{8,28},{12,0},{16,4},{20,8},{24,12},{28,16},{1,21},{... | collective-permute-start | bytes 15728648 | tf_op jit(solution)/shard_map/ppermute | solution.py:26
  837.3 2.4 copy-start
  839.6 788.2 %collective-permute-start.5 = (bf16[20,128,1024]{2,1,0:T(8,128)(2,1)}, bf16[20,128,1024]{2,1,0:T(8,128)(2,1)S(1)}, u32[]{:S(2)}, u32[]{:S(2)}) collective-permute-start(bf16[20,128,1024]{2,1,0:T(8,128)(2,1)} %get-tuple-element.12), channel_id=1, source_target_pairs={{0,24},{4,28},{8,0},{12,4},{16,8},{20,12},{24,16},{28,20},{1,25},{... | collective-permute-start | bytes 15728648 | tf_op jit(solution)/shard_map/ppermute | solution.py:26
  949.6 2.3 copy-start.1
  951.9 679.1 %collective-permute-start.6 = (bf16[20,128,1024]{2,1,0:T(8,128)(2,1)}, bf16[20,128,1024]{2,1,0:T(8,128)(2,1)S(1)}, u32[]{:S(2)}, u32[]{:S(2)}) collective-permute-start(bf16[20,128,1024]{2,1,0:T(8,128)(2,1)} %get-tuple-element.11), channel_id=1, source_target_pairs={{0,28},{4,0},{8,4},{12,8},{16,12},{20,16},{24,20},{28,24},{1,29},{... | collective-permute-start | bytes 15728648 | tf_op jit(solution)/shard_map/ppermute | solution.py:26
Sparse Core Ops, SparseCore 0:
  19.5 292.7 all-reduce.8
  330.6 71.9 all-reduce.4
  476.5 71.8 all-reduce.6
